TPU v7x, 256 devices: a whole 4x4x8 slice. The times are simulated.
256 devices in a mesh: dp: 32 (over z, y), ep: 8 (over x, core).
Axes of the slice: x: 4, y: 4, z: 8, core: 2. Of those that a mesh axis runs over, the one named last changes fastest.
Arguments:
- states: bfloat16 [2048, 16, 128, 128], P(('dp', 'ep')), may hold values from -4 to 4
- query_rows: bfloat16 [2048, 4, 1024], P(('dp', 'ep')), may hold values from -6 to 6
- key_rows: bfloat16 [2048, 4, 1024], P(('dp', 'ep')), may hold values from -6 to 6
- value_rows: bfloat16 [2048, 4, 2048], P(('dp', 'ep')), may hold values from -6 to 6
- gate_rows: bfloat16 [2048, 4, 2048], P(('dp', 'ep')), may hold values from -6 to 6
- beta_logit: bfloat16 [2048, 4, 16], P(('dp', 'ep')), may hold values from -6 to 6
- decay_logit: bfloat16 [2048, 4, 16], P(('dp', 'ep')), may hold values from -8 to 8
- residual: bfloat16 [2048, 4, 2048], P(('dp', 'ep')), may hold values from -6 to 6
- route_ids: int32 [2048, 4, 10], P(('dp', 'ep')), may hold values from 0 to 255, all different within a row; in each aligned block of 32 rows (0 to 31, 32 to 63, ..., all dimensions but the last counted through in order) at most 3 rows name the same one
- route_prob: float32 [2048, 4, 10], P(('dp', 'ep')), may hold values from 0.05 to 1
- out_weight: bfloat16 [2048, 2048], P(None, 'ep'), may hold values from -0.125 to 0.125
- core_gain: float32 [128], replicated, may hold values from 0.1 to 1.9
- moe_gain: float32 [2048], replicated, may hold values from 0.1 to 1.9
- gate_up: bfloat16 [256, 2048, 512], P(('dp', 'ep')), may hold values from -0.125 to 0.125
- down_weight: bfloat16 [256, 256, 2048], P(('dp', 'ep')), may hold values from -0.375 to 0.375
- new_home: int32 [2048], P(('dp', 'ep')), may hold values from 0 to 2047, as said below
Outputs:
- mixed_out: bfloat16 [2048, 4, 2048], P(('dp', 'ep'))
- moved_out: bfloat16 [2048, 16, 128, 128], P(('dp', 'ep'))
Inputs may be any that keep to these rules, and one draw needn't show every extreme that they name: `route_ids`: each row names 10 different experts; among the 32 rows of one device (its requests, each with its 4 tokens) no expert is named more than 3 times, a bound that some block reaches. `new_home`: A permutation of the request positions; a request stays among the 8 devices of its dp index, and every device hands exactly 1 of its requests to each device of that group, itself included.
All inputs are finite; a program needn't handle non-finite values.
Results may differ from a plain program's by a relative error of at most 0.01.
Values may be sent and summed in bfloat16 or wider, within the bound.
A program may use at most 128 MiB of HBM per device.

v0:
```python
import jax
import jax.numpy as jnp
from jax import lax
from jax.sharding import PartitionSpec as P

epsilon = 1e-06


def unit_rows(values):
    return values * lax.rsqrt(jnp.sum(values * values, -1, keepdims=True) + epsilon)


def delta_block(
    state_in, query_rows, key_rows, value_rows, gate_rows, beta_logit, decay_logit, core_gain
):
    batch_size = state_in.shape[0]
    head_count = decay_logit.shape[-1]
    head_width = state_in.shape[-1]
    key_heads = query_rows.shape[-1] // head_width
    repeats = head_count // key_heads
    memory_state = state_in.astype(jnp.float32)
    outputs = []
    for position in range(query_rows.shape[1]):
        queries = unit_rows(
            query_rows[:, position].astype(jnp.float32).reshape(batch_size, key_heads, head_width)
        )
        queries = jnp.repeat(queries, repeats, axis=1) * head_width ** (-0.5)
        key_units = unit_rows(
            key_rows[:, position].astype(jnp.float32).reshape(batch_size, key_heads, head_width)
        )
        key_units = jnp.repeat(key_units, repeats, axis=1)
        values = (
            value_rows[:, position].astype(jnp.float32).reshape(batch_size, head_count, head_width)
        )
        decays = jax.nn.sigmoid(decay_logit[:, position].astype(jnp.float32))
        strength = jax.nn.sigmoid(beta_logit[:, position].astype(jnp.float32))
        memory_state = memory_state * decays[:, :, None, None]
        memory = jnp.einsum(
            "bhkv,bhk->bhv", memory_state, key_units, precision=lax.Precision.HIGHEST
        )
        update = (values - memory) * strength[:, :, None]
        memory_state = memory_state + key_units[:, :, :, None] * update[:, :, None, :]
        reading = jnp.einsum(
            "bhkv,bhk->bhv", memory_state, queries, precision=lax.Precision.HIGHEST
        )
        scaled = reading * lax.rsqrt(jnp.mean(reading * reading, -1, keepdims=True) + epsilon)
        gate_vals = (
            gate_rows[:, position].astype(jnp.float32).reshape(batch_size, head_count, head_width)
        )
        gated_out = scaled * core_gain * jax.nn.silu(gate_vals)
        outputs.append(gated_out.reshape(batch_size, head_count * head_width).astype(jnp.bfloat16))
    return (memory_state.astype(jnp.bfloat16), jnp.stack(outputs, axis=1))


def rms_scale(values, gain):
    return values * lax.rsqrt(jnp.mean(values * values, -1, keepdims=True) + epsilon) * gain


def expert_apply(chosen_rows, gate_up, down_weight):
    hidden_units = down_weight.shape[0]
    joined = jnp.dot(chosen_rows, gate_up, preferred_element_type=jnp.float32)
    active = (jax.nn.silu(joined[:, :hidden_units]) * joined[:, hidden_units:]).astype(jnp.bfloat16)
    return jnp.dot(active, down_weight, preferred_element_type=jnp.float32).astype(jnp.bfloat16)


def pack(values, positions, lane_count):
    zeroed = jnp.zeros(values.shape, values.dtype)
    placed = zeroed.at[positions].set(values)
    return placed.reshape((lane_count, values.shape[0] // lane_count) + values.shape[1:])


def unpack(values):
    return values.reshape((values.shape[0] * values.shape[1],) + values.shape[2:])


def shards(
    states,
    query_rows,
    key_rows,
    value_rows,
    gate_rows,
    beta_logit,
    decay_logit,
    residual,
    route_ids,
    route_prob,
    out_weight,
    core_gain,
    moe_gain,
    gate_up,
    down_weight,
    new_home,
):
    req_count = states.shape[0]
    step_count = query_rows.shape[1]
    model_width = residual.shape[-1]
    ep_size = lax.axis_size("ep")
    dp_size = lax.axis_size("dp")
    target = new_home // req_count % ep_size
    new_place = new_home % req_count
    order_ids = jnp.arange(req_count, dtype=jnp.int32)
    earlier = (target[:, None] == target[None, :]) & (order_ids[None, :] < order_ids[:, None])
    lane_rank = jnp.sum(earlier.astype(jnp.int32), axis=1)
    lane_cap = req_count // ep_size
    buffer_index = target * lane_cap + lane_rank
    fresh_states, core_out = delta_block(
        states, query_rows, key_rows, value_rows, gate_rows, beta_logit, decay_logit, core_gain
    )
    received = (
        lax.all_to_all(
            pack(fresh_states, buffer_index, ep_size), "ep", split_axis=0, concat_axis=0, tiled=True
        ),
        lax.all_to_all(
            pack(new_place, buffer_index, ep_size), "ep", split_axis=0, concat_axis=0, tiled=True
        ),
    )
    moved_out = jnp.zeros_like(states).at[unpack(received[1])].set(unpack(received[0]), mode="drop")
    token_count = req_count * step_count
    core_flat = core_out.reshape(token_count, core_out.shape[-1])
    columns = jnp.dot(
        lax.all_gather(core_flat, "ep", axis=0, tiled=True),
        out_weight,
        preferred_element_type=jnp.float32,
    ).astype(jnp.bfloat16)
    attention = lax.all_to_all(columns, "ep", split_axis=0, concat_axis=1, tiled=True)
    hidden = (
        residual.reshape(token_count, model_width).astype(jnp.float32)
        + attention.astype(jnp.float32)
    ).astype(jnp.bfloat16)
    normed = rms_scale(hidden.astype(jnp.float32), moe_gain).astype(jnp.bfloat16)
    top_count = route_ids.shape[-1]
    experts = dp_size * ep_size
    capacity = (token_count * top_count + experts - 1) // experts + 1
    flat_ids = route_ids.reshape(-1)
    onehot = (flat_ids[:, None] == jnp.arange(experts, dtype=jnp.int32)[None, :]).astype(jnp.int32)
    route_rank = jnp.sum(jnp.cumsum(onehot, axis=0) * onehot, axis=1) - 1
    slot_index = flat_ids * capacity + route_rank
    outgoing = (
        jnp.zeros((experts * capacity, model_width), jnp.bfloat16)
        .at[slot_index]
        .set(jnp.repeat(normed, top_count, axis=0))
    )
    arrived = lax.all_to_all(
        lax.all_to_all(
            outgoing.reshape(dp_size, ep_size, capacity, model_width),
            "dp",
            split_axis=0,
            concat_axis=0,
            tiled=True,
        ),
        "ep",
        split_axis=1,
        concat_axis=1,
        tiled=True,
    )
    result = expert_apply(arrived.reshape(-1, model_width), gate_up[0], down_weight[0]).reshape(
        dp_size, ep_size, capacity, model_width
    )
    returned = lax.all_to_all(
        lax.all_to_all(result, "dp", split_axis=0, concat_axis=0, tiled=True),
        "ep",
        split_axis=1,
        concat_axis=1,
        tiled=True,
    )
    routed = returned.reshape(experts * capacity, model_width)[slot_index]
    weights = route_prob.reshape(token_count, top_count)
    weights = weights / jnp.sum(weights, -1, keepdims=True)
    combined = jnp.sum(
        routed.reshape(token_count, top_count, model_width).astype(jnp.float32)
        * weights[:, :, None],
        axis=1,
    )
    mixed_out = (
        (hidden.astype(jnp.float32) + combined)
        .astype(jnp.bfloat16)
        .reshape(req_count, step_count, model_width)
    )
    return (mixed_out, moved_out)


def solution(mesh):
    placed = (
        P(("dp", "ep"), None, None, None),
        P(("dp", "ep"), None, None),
        P(("dp", "ep"), None, None),
        P(("dp", "ep"), None, None),
        P(("dp", "ep"), None, None),
        P(("dp", "ep"), None, None),
        P(("dp", "ep"), None, None),
        P(("dp", "ep"), None, None),
        P(("dp", "ep"), None, None),
        P(("dp", "ep"), None, None),
        P(None, "ep"),
        P(),
        P(),
        P(("dp", "ep"), None, None),
        P(("dp", "ep"), None, None),
        P(("dp", "ep")),
    )
    return jax.shard_map(
        shards,
        mesh=mesh,
        in_specs=placed,
        out_specs=(P(("dp", "ep"), None, None), P(("dp", "ep"), None, None, None)),
        check_vma=False,
    )
```

profile of v0, /device:TPU:24, one launch (start us, length us, event | category | flops | bytes accessed | tf_op | source)
XLA Modules:
  0.0 571.1 jit_solution(461292190551067246)
XLA Ops:
  7.2 0.9 fusion.58
  8.1 0.9 fusion.59
  9.0 1.2 slice_convert_fusion.14
  10.9 1.1 slice_convert_fusion.15
  12.8 1.5 slice_convert_fusion.7
  14.3 9.7 %fusion = f32[8,16,1,128]{3,2,1,0:T(1,128)S(1)} fusion(f32[8,16,128,1]{2,3,1,0:T(1,128)S(1)} %bitcast.152, bf16[8,16,128,128]{3,2,1,0:T(8,128)(2,1)} %param.16, f32[8,16]{1,0:T(8,128)S(1)} %get-tuple-element.37), kind=kOutput, calls=%fused_computation.10 | convolution fusion | flops 29360128 | bytes 4325888 | tf_op jit(solution)/shard_map/bhkv,bhk->bhv/dot_general | solution.py:38
  24.1 8.3 %fusion.2 = f32[8,16,1,128]{3,2,1,0:T(1,128)S(1)} fusion(f32[8,16,128,1]{2,3,1,0:T(1,128)S(1)} %bitcast.196, bf16[8,16,128,128]{3,2,1,0:T(8,128)(2,1)S(1)} %copy-done.1, f32[8,16,128]{2,1,0:T(8,128)S(1)} %subtract_multiply_fusion.3, f32[8,16,128]{2,1,0:T(8,128)S(1)} %bitcast.153, f32[8,16]{1,0:T(8,128)S(1)} %get-tuple-element.37), kind=kOutput, calls=%fused_computation.12 | convolution fusion | flops 33554432 | bytes 4456960 | tf_op jit(solution)/shard_map/bhkv,bhk->bhv/dot_general | solution.py:43
  32.6 9.0 %fusion.3 = f32[8,16,1,128]{3,2,1,0:T(1,128)S(1)} fusion(f32[8,16,128,1]{2,3,1,0:T(1,128)S(1)} %bitcast.161, bf16[8,16,128,128]{3,2,1,0:T(8,128)(2,1)S(1)} %copy-done.1, f32[8,16]{1,0:T(8,128)S(1)} %get-tuple-element.36, f32[8,16,128]{2,1,0:T(8,128)S(1)} %subtract_multiply_fusion.3, f32[8,16,128]{2,1,0:T(8,128)S(1)} %bitcast.154, ...), kind=kOutput, calls=%fused_computation.13 | convolution fusion | flops 35651584 | bytes 4457472 | tf_op jit(solution)/shard_map/bhkv,bhk->bhv/dot_general | solution.py:38
  41.7 11.6 %fusion.11 = f32[8,16,1,128]{3,2,1,0:T(1,128)S(1)} fusion(f32[8,16,128,1]{2,3,1,0:T(1,128)S(1)} %bitcast.197, bf16[8,16,128,128]{3,2,1,0:T(8,128)(2,1)S(1)} %copy-done.1, f32[8,16,128]{2,1,0:T(8,128)S(1)} %subtract_multiply_fusion.2, f32[8,16,128]{2,1,0:T(8,128)S(1)} %bitcast.162, f32[8,16]{1,0:T(8,128)S(1)} %get-tuple-element.36, ...), kind=kOutput, calls=%fused_computation.20 | convolution fusion | flops 39845888 | bytes 4588544 | tf_op jit(solution)/shard_map/bhkv,bhk->bhv/dot_general | solution.py:43
  53.4 11.7 %fusion.7 = f32[8,16,1,128]{3,2,1,0:T(1,128)S(1)} fusion(f32[8,16,128,1]{2,3,1,0:T(1,128)S(1)} %bitcast.168, bf16[8,16,128,128]{3,2,1,0:T(8,128)(2,1)S(1)} %copy-done.1, f32[8,16]{1,0:T(8,128)S(1)} %get-tuple-element.35, f32[8,16,128]{2,1,0:T(8,128)S(1)} %subtract_multiply_fusion.2, f32[8,16,128]{2,1,0:T(8,128)S(1)} %bitcast.163, ...), kind=kOutput, calls=%fused_computation.16 | convolution fusion | flops 41943040 | bytes 4589056 | tf_op jit(solution)/shard_map/bhkv,bhk->bhv/dot_general | solution.py:38
  65.2 15.5 %fusion.43 = f32[8,16,1,128]{3,2,1,0:T(1,128)S(1)} fusion(f32[8,16,128,1]{2,3,1,0:T(1,128)S(1)} %bitcast.198, bf16[8,16,128,128]{3,2,1,0:T(8,128)(2,1)S(1)} %copy-done.1, f32[8,16,128]{2,1,0:T(8,128)S(1)} %subtract_multiply_fusion.1, f32[8,16,128]{2,1,0:T(8,128)S(1)} %bitcast.169, f32[8,16]{1,0:T(8,128)S(1)} %get-tuple-element.35, ...), kind=kOutput, calls=%fused_computation.56 | convolution fusion | flops 46137344 | bytes 4720128 | tf_op jit(solution)/shard_map/bhkv,bhk->bhv/dot_general | solution.py:43
  80.9 15.6 %fusion.5 = f32[8,16,1,128]{3,2,1,0:T(1,128)S(1)} fusion(f32[8,16,128,1]{2,3,1,0:T(1,128)S(1)} %bitcast.173, f32[8,16]{1,0:T(8,128)S(1)} %get-tuple-element.34, bf16[8,16,128,128]{3,2,1,0:T(8,128)(2,1)S(1)} %copy-done.1, f32[8,16,128]{2,1,0:T(8,128)S(1)} %subtract_multiply_fusion.1, f32[8,16,128]{2,1,0:T(8,128)S(1)} %bitcast.170, ...), kind=kOutput, calls=%fused_computation.14 | convolution fusion | flops 48234496 | bytes 4720640 | tf_op jit(solution)/shard_map/bhkv,bhk->bhv/dot_general | solution.py:38
  96.8 21.1 %fusion.10 = f32[8,16,1,128]{3,2,1,0:T(1,128)S(1)} fusion(f32[8,16,128,1]{2,3,1,0:T(1,128)S(1)} %bitcast.199, f32[8,16,128]{2,1,0:T(8,128)S(1)} %subtract_multiply_fusion, f32[8,16,128]{2,1,0:T(8,128)S(1)} %bitcast.174, f32[8,16]{1,0:T(8,128)S(1)} %get-tuple-element.34, bf16[8,16,128,128]{3,2,1,0:T(8,128)(2,1)S(1)} %copy-done.1, ...), kind=kOutput, calls=%fused_computation.19 | convolution fusion | flops 52428800 | bytes 4851712 | tf_op jit(solution)/shard_map/bhkv,bhk->bhv/dot_general | solution.py:43
  118.0 0.2 slice_convert_fusion.6
  118.7 0.7 reshape.500
  119.7 0.3 fusion.44
  120.2 0.2 fusion.48
  120.4 27.7 %all-gather.2.cloned.1.call-done = bf16[256,2048]{1,0:T(8,128)(2,1)} async-done(((bf16[32,2048]{1,0:T(8,128)(2,1)}), bf16[256,2048]{1,0:T(8,128)(2,1)}) %all-gather.2.cloned.1.call-update) | async-done | bytes 1048592 | tf_op jit(solution)/shard_map/all_gather | solution.py:121
  148.1 2.6 convolution_convert_fusion.1
  150.7 3.5 all-to-all-start
  154.5 0.6 fusion.52
  155.1 5.3 all-to-all-done
  160.4 0.2 copy.100
  160.7 0.2 fusion.49
  161.0 0.8 multiply_convert_fusion
  161.8 1.6 broadcast_in_dim.31
  163.4 3.6 reshape.560
  166.9 5.4 scatter_custom_fusion
  172.3 9.1 %reshape.504 = bf16[32,8,3,2048]{3,2,1,0:T(4,128)(2,1)} reshape(bf16[768,2048]{1,0:T(8,128)(2,1)} %scatter_custom_fusion) | data formatting | bytes 6291456 | tf_op jit(solution)/shard_map/reshape | solution.py:145
  181.4 5.5 copy.104
  186.9 82.7 %all_to_all.50 = bf16[32,8,3,2048]{3,1,2,0:T(8,128)(2,1)S(1)} all-to-all(bf16[32,8,3,2048]{3,1,2,0:T(8,128)(2,1)S(1)} %copy.104), channel_id=1, replica_groups=mesh['dp'=32,'ep'=8] {'dp'}, dimensions={0} | all-to-all | bytes 6291456 | tf_op jit(solution)/shard_map/all_to_all | solution.py:144
  269.7 3.4 copy.105
  273.1 4.6 all-to-all-start.2
  277.7 0.2 convert_reduce_fusion
  277.9 0.6 scatter_custom_fusion.1
  278.5 0.7 copy.110
  279.1 36.9 %all-to-all-done.2 = bf16[32,8,3,2048]{3,0,2,1:T(8,128)(2,1)} async-done(((bf16[32,8,3,2048]{3,0,2,1:T(8,128)(2,1)}), bf16[32,8,3,2048]{3,0,2,1:T(8,128)(2,1)}, u32[]{:S(2)}, u32[]{:S(2)}) %all-to-all-start.2) | async-done | bytes 3145760 | tf_op jit(solution)/shard_map/all_to_all | solution.py:143
  316.1 3.5 all-to-all-start.5
  319.6 6.6 %copy.106 = bf16[32,8,3,2048]{3,2,1,0:T(4,128)(2,1)} copy(bf16[32,8,3,2048]{3,0,2,1:T(8,128)(2,1)} %all-to-all-done.2) | data formatting | bytes 6291456 | tf_op jit(solution)/shard_map/all_to_all | solution.py:143
  326.2 8.8 %reshape.505 = bf16[768,2048]{1,0:T(8,128)(2,1)} reshape(bf16[32,8,3,2048]{3,2,1,0:T(4,128)(2,1)} %copy.106) | data formatting | bytes 6291456 | tf_op jit(solution)/shard_map/reshape | solution.py:156
  335.0 3.8 fusion.37
  338.8 2.7 convolution_convert_fusion
  341.5 9.1 %reshape.506 = bf16[32,8,3,2048]{3,2,1,0:T(4,128)(2,1)} reshape(bf16[768,2048]{1,0:T(8,128)(2,1)} %convolution_convert_fusion) | data formatting | bytes 6291456 | tf_op jit(solution)/shard_map/reshape | solution.py:156
  350.6 7.2 %copy.107 = bf16[32,8,3,2048]{3,1,2,0:T(8,128)(2,1)} copy(bf16[32,8,3,2048]{3,2,1,0:T(4,128)(2,1)} %reshape.506) | data formatting | bytes 6291456 | tf_op jit(solution)/shard_map/reshape | solution.py:156
  357.9 5.8 %all-to-all-start.3 = ((bf16[32,8,3,2048]{3,1,2,0:T(8,128)(2,1)}), bf16[32,8,3,2048]{3,1,2,0:T(8,128)(2,1)}, u32[]{:S(2)}, u32[]{:S(2)}) async-start(bf16[32,8,3,2048]{3,1,2,0:T(8,128)(2,1)} %copy.107), calls=%async_computation.3 | async-start | bytes 6291456 | tf_op jit(solution)/shard_map/all_to_all | solution.py:160
  363.7 13.3 %fusion.9 = bf16[8,16,128,128]{3,2,1,0:T(8,128)(2,1)} fusion(f32[8,16,128]{2,1,0:T(8,128)S(1)} %copy-done.13, f32[8,16,128]{2,1,0:T(8,128)S(1)} %bitcast.175, f32[8,16]{1,0:T(8,128)S(1)} %get-tuple-element.34, f32[8,16,128]{2,1,0:T(8,128)S(1)} %copy-done.11, f32[8,16,128]{2,1,0:T(8,128)S(1)} %bitcast.172, f32[8,16]{1,0:T(8,128)S(1)} %get-tuple-element.35, ...), kind=kLoop, calls=%fused_computation.18 | loop fusion | flops 29360128 | bytes 8914944 | tf_op jit(solution)/shard_map/convert_element_type | solution.py:52
  377.0 3.1 broadcast.332.clone
  380.0 10.9 %scatter_fusion = bf16[8,16,128,128]{3,2,1,0:T(8,128)(2,1)} fusion(bf16[8,16,128,128]{3,2,1,0:T(8,128)(2,1)} %broadcast.332.clone, s32[8]{0:T(128)S(1)} %compare_select_fusion.2, bf16[8,16,128,128]{3,2,1,0:T(8,128)(2,1)} %fusion.9), kind=kCustom, calls=%fused_computation.3 | custom fusion | bytes 12582944 | tf_op jit(solution)/shard_map/scatter | solution.py:68
  390.9 46.9 %all-to-all-done.3 = bf16[32,8,3,2048]{3,1,2,0:T(8,128)(2,1)} async-done(((bf16[32,8,3,2048]{3,1,2,0:T(8,128)(2,1)}), bf16[32,8,3,2048]{3,1,2,0:T(8,128)(2,1)}, u32[]{:S(2)}, u32[]{:S(2)}) %all-to-all-start.3) | async-done | bytes 3145760 | tf_op jit(solution)/shard_map/all_to_all | solution.py:160
  437.7 4.8 all-to-all-start.6
  442.5 5.3 copy.108
  447.9 44.3 %all-to-all-done.6 = bf16[8,1,16,128,128]{4,3,2,1,0:T(8,128)(2,1)} async-done(((bf16[8,1,16,128,128]{4,3,2,1,0:T(8,128)(2,1)}), bf16[8,1,16,128,128]{4,3,2,1,0:T(8,128)(2,1)}, u32[]{:S(2)}, u32[]{:S(2)}) %all-to-all-start.6) | async-done | bytes 4194336 | tf_op jit(solution)/shard_map/all_to_all | solution.py:110
  492.2 4.5 all-to-all-start.4
  496.9 0.6 pad_clamp_fusion
  497.5 0.2 reduce.3
  497.8 3.1 broadcast.332
  500.8 10.9 %scatter_fusion.1 = bf16[8,16,128,128]{3,2,1,0:T(8,128)(2,1)} fusion(bf16[8,16,128,128]{3,2,1,0:T(8,128)(2,1)} %broadcast.332, s32[8]{0:T(128)S(1)} %fusion.54, bf16[8,16,128,128]{3,2,1,0:T(8,128)(2,1)} %bitcast.77), kind=kCustom, calls=%fused_computation.4 | custom fusion | bytes 12582944 | tf_op jit(solution)/shard_map/scatter | solution.py:117
  511.7 23.4 %all-to-all-done.4 = bf16[32,8,3,2048]{3,0,2,1:T(8,128)(2,1)} async-done(((bf16[32,8,3,2048]{3,0,2,1:T(8,128)(2,1)}), bf16[32,8,3,2048]{3,0,2,1:T(8,128)(2,1)}, u32[]{:S(2)}, u32[]{:S(2)}) %all-to-all-start.4) | async-done | bytes 3145760 | tf_op jit(solution)/shard_map/all_to_all | solution.py:159
  535.1 6.5 %copy.109 = bf16[32,8,3,2048]{3,2,1,0:T(4,128)(2,1)} copy(bf16[32,8,3,2048]{3,0,2,1:T(8,128)(2,1)} %all-to-all-done.4) | data formatting | bytes 6291456 | tf_op jit(solution)/shard_map/all_to_all | solution.py:159
  541.6 8.8 %reshape.507 = bf16[768,2048]{1,0:T(8,128)(2,1)} reshape(bf16[32,8,3,2048]{3,2,1,0:T(4,128)(2,1)} %copy.109) | data formatting | bytes 6291456 | tf_op jit(solution)/shard_map/reshape | solution.py:166
  550.4 6.8 %gather_fusion = bf16[320,2048]{1,0:T(8,128)(2,1)S(1)} fusion(bf16[768,2048]{1,0:T(8,128)(2,1)} %reshape.507, s32[1024]{0:T(1024)} %pad_clamp_fusion), kind=kCustom, calls=%fused_computation | custom fusion | bytes 2622720 | tf_op jit(solution)/shard_map/gather | solution.py:166
  557.2 2.1 reshape.547
  559.4 3.6 multiply_reduce_fusion
  563.1 0.8 fusion.50
  (137 shorter events, 4.1 us)
Async XLA Ops:
  7.2 327.9 %copy-start = (bf16[1,2048,512]{2,1,0:T(8,128)(2,1)S(1)}, bf16[1,2048,512]{2,1,0:T(8,128)(2,1)}, u32[]{:S(2)}) copy-start(bf16[1,2048,512]{2,1,0:T(8,128)(2,1)} %param.29) | copy-start | bytes 6291460
  7.2 140.9 %all-gather.2.cloned.1.call-start = ((), (), s32[]{:S(2)}) async-start(), calls=%async_computation.7 | async-start | bytes 1179648 | tf_op jit(solution)/shard_map/all_gather | solution.py:121
  9.0 15.1 %copy-start.1 = (bf16[8,16,128,128]{3,2,1,0:T(8,128)(2,1)S(1)}, bf16[8,16,128,128]{3,2,1,0:T(8,128)(2,1)}, u32[]{:S(2)}) copy-start(bf16[8,16,128,128]{3,2,1,0:T(8,128)(2,1)} %param.16) | copy-start | bytes 12582916
  14.3 82.4 %copy-start.14 = (f32[8,8,2,128]{3,2,1,0:T(2,128)}, f32[8,8,2,128]{3,2,1,0:T(2,128)S(1)}, u32[]{:S(2)}) copy-start(f32[8,8,2,128]{3,2,1,0:T(2,128)S(1)} %broadcast_in_dim.22) | copy-start | bytes 196612
  24.1 72.6 %copy-start.6 = (f32[8,16,128]{2,1,0:T(8,128)}, f32[8,16,128]{2,1,0:T(8,128)S(1)}, u32[]{:S(2)}) copy-start(f32[8,16,128]{2,1,0:T(8,128)S(1)} %subtract_multiply_fusion.3) | copy-start | bytes 196612
  32.6 64.1 %copy-start.16 = (f32[8,8,2,128]{3,2,1,0:T(2,128)}, f32[8,8,2,128]{3,2,1,0:T(2,128)S(1)}, u32[]{:S(2)}) copy-start(f32[8,8,2,128]{3,2,1,0:T(2,128)S(1)} %broadcast_in_dim.24) | copy-start | bytes 196612
  41.6 55.1 %copy-start.8 = (f32[8,16,128]{2,1,0:T(8,128)}, f32[8,16,128]{2,1,0:T(8,128)S(1)}, u32[]{:S(2)}) copy-start(f32[8,16,128]{2,1,0:T(8,128)S(1)} %subtract_multiply_fusion.2) | copy-start | bytes 196612
  53.4 43.3 %copy-start.18 = (f32[8,8,2,128]{3,2,1,0:T(2,128)}, f32[8,8,2,128]{3,2,1,0:T(2,128)S(1)}, u32[]{:S(2)}) copy-start(f32[8,8,2,128]{3,2,1,0:T(2,128)S(1)} %broadcast_in_dim.26) | copy-start | bytes 196612
  65.2 31.5 %copy-start.10 = (f32[8,16,128]{2,1,0:T(8,128)}, f32[8,16,128]{2,1,0:T(8,128)S(1)}, u32[]{:S(2)}) copy-start(f32[8,16,128]{2,1,0:T(8,128)S(1)} %subtract_multiply_fusion.1) | copy-start | bytes 196612
  80.9 15.8 %copy-start.20 = (f32[8,8,2,128]{3,2,1,0:T(2,128)}, f32[8,8,2,128]{3,2,1,0:T(2,128)S(1)}, u32[]{:S(2)}) copy-start(f32[8,8,2,128]{3,2,1,0:T(2,128)S(1)} %broadcast_in_dim.28) | copy-start | bytes 196612
  96.6 21.3 %copy-start.12 = (f32[8,16,128]{2,1,0:T(8,128)}, f32[8,16,128]{2,1,0:T(8,128)S(1)}, u32[]{:S(2)}) copy-start(f32[8,16,128]{2,1,0:T(8,128)S(1)} %subtract_multiply_fusion) | copy-start | bytes 196612
  96.7 21.3 %copy-start.5 = (bf16[8,4,2048]{2,1,0:T(4,128)(2,1)S(1)}, bf16[8,4,2048]{2,1,0:T(4,128)(2,1)}, u32[]{:S(2)}) copy-start(bf16[8,4,2048]{2,1,0:T(4,128)(2,1)} %param.20) | copy-start | bytes 393220
  96.8 21.5 %copy-start.25 = (f32[128]{0:T(128)S(1)}, f32[128]{0:T(128)}, u32[]{:S(2)}) copy-start(f32[128]{0:T(128)} %param.27) | copy-start | bytes 1540
  96.8 22.6 %copy-start.22 = (s32[8,4,10]{2,1,0:T(4,128)S(1)}, s32[8,4,10]{2,1,0:T(4,128)}, u32[]{:S(2)}) copy-start(s32[8,4,10]{2,1,0:T(4,128)} %param.24) | copy-start | bytes 3844
  118.2 36.2 %copy-start.4 = (bf16[8,4,2048]{2,1,0:T(4,128)(2,1)S(1)}, bf16[8,4,2048]{2,1,0:T(4,128)(2,1)}, u32[]{:S(2)}) copy-start(bf16[8,4,2048]{2,1,0:T(4,128)(2,1)} %param.23) | copy-start | bytes 393220
  150.7 9.6 %all-to-all-start = ((bf16[8,32,256]{2,1,0:T(8,128)(2,1)}), bf16[8,32,256]{2,1,0:T(8,128)(2,1)S(1)}, u32[]{:S(2)}, u32[]{:S(2)}) async-start(bf16[8,32,256]{2,1,0:T(8,128)(2,1)} %bitcast.64), calls=%async_computation | async-start | bytes 262144 | tf_op jit(solution)/shard_map/all_to_all | solution.py:125
  160.7 11.7 %copy-start.2 = (f32[8,4,2048]{2,1,0:T(4,128)}, f32[8,4,2048]{2,1,0:T(4,128)S(1)}, u32[]{:S(2)}) copy-start(f32[8,4,2048]{2,1,0:T(4,128)S(1)} %reshape.543) | copy-start | bytes 786436
  273.1 4.6 copy-start.27
  273.1 43.0 %all-to-all-start.2 = ((bf16[32,8,3,2048]{3,0,2,1:T(8,128)(2,1)}), bf16[32,8,3,2048]{3,0,2,1:T(8,128)(2,1)}, u32[]{:S(2)}, u32[]{:S(2)}) async-start(bf16[32,8,3,2048]{3,0,2,1:T(8,128)(2,1)} %copy.105), calls=%async_computation.2 | async-start | bytes 6291456 | tf_op jit(solution)/shard_map/all_to_all | solution.py:143
  316.1 41.8 %all-to-all-start.5 = ((s32[8,1,1]{2,1,0:T(1,128)}), s32[8,1,1]{2,1,0:T(1,128)S(1)}, u32[]{:S(2)}, u32[]{:S(2)}) async-start(s32[8,1,1]{2,1,0:T(1,128)} %copy.110), calls=%async_computation.5 | async-start | bytes 8192 | tf_op jit(solution)/shard_map/all_to_all | solution.py:113
  335.0 3.8 copy-start.26
  357.8 5.8 %copy-start.7 = (f32[8,16,128]{2,1,0:T(8,128)S(1)}, f32[8,16,128]{2,1,0:T(8,128)}, u32[]{:S(2)}) copy-start(f32[8,16,128]{2,1,0:T(8,128)} %copy-done.6) | copy-start | bytes 196612
  357.8 5.8 %copy-start.9 = (f32[8,16,128]{2,1,0:T(8,128)S(1)}, f32[8,16,128]{2,1,0:T(8,128)}, u32[]{:S(2)}) copy-start(f32[8,16,128]{2,1,0:T(8,128)} %copy-done.8) | copy-start | bytes 196612
  357.8 5.8 %copy-start.11 = (f32[8,16,128]{2,1,0:T(8,128)S(1)}, f32[8,16,128]{2,1,0:T(8,128)}, u32[]{:S(2)}) copy-start(f32[8,16,128]{2,1,0:T(8,128)} %copy-done.10) | copy-start | bytes 196612
  357.8 5.9 %copy-start.13 = (f32[8,16,128]{2,1,0:T(8,128)S(1)}, f32[8,16,128]{2,1,0:T(8,128)}, u32[]{:S(2)}) copy-start(f32[8,16,128]{2,1,0:T(8,128)} %copy-done.12) | copy-start | bytes 196612
  357.8 5.9 %copy-start.15 = (f32[8,8,2,128]{3,2,1,0:T(2,128)S(1)}, f32[8,8,2,128]{3,2,1,0:T(2,128)}, u32[]{:S(2)}) copy-start(f32[8,8,2,128]{3,2,1,0:T(2,128)} %copy-done.14) | copy-start | bytes 196612
  357.8 5.9 %copy-start.17 = (f32[8,8,2,128]{3,2,1,0:T(2,128)S(1)}, f32[8,8,2,128]{3,2,1,0:T(2,128)}, u32[]{:S(2)}) copy-start(f32[8,8,2,128]{3,2,1,0:T(2,128)} %copy-done.16) | copy-start | bytes 196612
  357.8 5.9 %copy-start.19 = (f32[8,8,2,128]{3,2,1,0:T(2,128)S(1)}, f32[8,8,2,128]{3,2,1,0:T(2,128)}, u32[]{:S(2)}) copy-start(f32[8,8,2,128]{3,2,1,0:T(2,128)} %copy-done.18) | copy-start | bytes 196612
  357.8 5.9 %copy-start.21 = (f32[8,8,2,128]{3,2,1,0:T(2,128)S(1)}, f32[8,8,2,128]{3,2,1,0:T(2,128)}, u32[]{:S(2)}) copy-start(f32[8,8,2,128]{3,2,1,0:T(2,128)} %copy-done.20) | copy-start | bytes 196612
  357.9 79.9 %all-to-all-start.3 = ((bf16[32,8,3,2048]{3,1,2,0:T(8,128)(2,1)}), bf16[32,8,3,2048]{3,1,2,0:T(8,128)(2,1)}, u32[]{:S(2)}, u32[]{:S(2)}) async-start(bf16[32,8,3,2048]{3,1,2,0:T(8,128)(2,1)} %copy.107), calls=%async_computation.3 | async-start | bytes 6291456 | tf_op jit(solution)/shard_map/all_to_all | solution.py:160
  437.7 54.5 %all-to-all-start.6 = ((bf16[8,1,16,128,128]{4,3,2,1,0:T(8,128)(2,1)}), bf16[8,1,16,128,128]{4,3,2,1,0:T(8,128)(2,1)}, u32[]{:S(2)}, u32[]{:S(2)}) async-start(bf16[8,1,16,128,128]{4,3,2,1,0:T(8,128)(2,1)} %bitcast.132), calls=%async_computation.6 | async-start | bytes 8388608 | tf_op jit(solution)/shard_map/all_to_all | solution.py:110
  447.9 48.8 %copy-start.23 = (f32[8,4,10]{2,1,0:T(4,128)S(1)}, f32[8,4,10]{2,1,0:T(4,128)}, u32[]{:S(2)}) copy-start(f32[8,4,10]{2,1,0:T(4,128)} %param.25) | copy-start | bytes 3844
  447.9 49.0 %copy-start.24 = (s32[320]{0:T(512)S(1)}, s32[320]{0:T(512)}, u32[]{:S(2)}) copy-start(s32[320]{0:T(512)} %fusion.52) | copy-start | bytes 3844
  492.2 42.9 %all-to-all-start.4 = ((bf16[32,8,3,2048]{3,0,2,1:T(8,128)(2,1)}), bf16[32,8,3,2048]{3,0,2,1:T(8,128)(2,1)}, u32[]{:S(2)}, u32[]{:S(2)}) async-start(bf16[32,8,3,2048]{3,0,2,1:T(8,128)(2,1)} %copy.108), calls=%async_computation.4 | async-start | bytes 6291456 | tf_op jit(solution)/shard_map/all_to_all | solution.py:159
  559.4 3.7 copy-start.3
Sparse Core Ops, SparseCore 0:
  119.5 28.5 all-gather.1
where the time goes:
time: 577 us; the launch traced here: 571 us
  waiting for transfers between devices  185 us (32%)
  local copies, waits for them, and re-layouts  123 us (21%)
  matrix products  112 us (19%)
  blocking collectives  82.7 us (14%)
  other arithmetic  27.5 us (5%)
  starting transfers between devices  26.7 us (5%)
  between operations  15.4 us (3%)
    all_to_all x1, blocking collectives, shards(): lax.all_to_all(outgoing.reshape(dp_size, ep_size, capacity, model_width),...  82.7 us
    dot_general x4, matrix products, delta_block(): jnp.einsum('bhkv,bhk->bhv', memory_state, queries, precision=lax.Precisio...  56.5 us
    all_to_all x1, waiting for transfers between devices, shards(): lax.all_to_all(result, 'dp', split_axis=0, concat_axis=0, tiled=True)  46.9 us
    dot_general x4, matrix products, delta_block(): jnp.einsum('bhkv,bhk->bhv', memory_state, key_units, precision=lax.Precis...  45.9 us
    all_to_all x1, waiting for transfers between devices, shards(): lax.all_to_all(pack(fresh_states, buffer_index, ep_size), 'ep', split_axi...  44.3 us
    all_to_all x1, waiting for transfers between devices, shards(): lax.all_to_all(lax.all_to_all(outgoing.reshape(dp_size, ep_size, capacity...  36.9 us
    all_gather x1, waiting for transfers between devices, shards(): lax.all_gather(core_flat, 'ep', axis=0, tiled=True)  27.7 us
    all_to_all x1, waiting for transfers between devices, shards(): lax.all_to_all(lax.all_to_all(result, 'dp', split_axis=0, concat_axis=0,...  23.4 us
  transfers between devices with their start and end apart: 7, of which 6 were waited for; matrix products, arithmetic and copies ran while one was open for 16% of the time, Pallas kernels for 0%

commit v1 on v0

--- a/solution.py
+++ b/solution.py
@@ -4,6 +4,14 @@
 from jax.sharding import PartitionSpec as P
 
 epsilon = 1e-06
+
+
+def gather_by_exchange(shard, axis, dim):
+    size = lax.axis_size(axis)
+    repeats = [size if d == dim else 1 for d in range(shard.ndim)]
+    return lax.all_to_all(
+        jnp.tile(shard, repeats), axis, split_axis=dim, concat_axis=dim, tiled=True
+    )
 
 
 def unit_rows(values):
@@ -118,9 +126,7 @@
     token_count = req_count * step_count
     core_flat = core_out.reshape(token_count, core_out.shape[-1])
     columns = jnp.dot(
-        lax.all_gather(core_flat, "ep", axis=0, tiled=True),
-        out_weight,
-        preferred_element_type=jnp.float32,
+        gather_by_exchange(core_flat, "ep", 0), out_weight, preferred_element_type=jnp.float32
     ).astype(jnp.bfloat16)
     attention = lax.all_to_all(columns, "ep", split_axis=0, concat_axis=1, tiled=True)
     hidden = (

time: 577 us -> 557 us (0.965)
  waiting for transfers between devices: 185 us -> 170 us
  between operations: 15.4 us -> 1.99 us
    all_gather x1 -> x0, waiting for transfers between devices: 27.7 us -> none  [shards(): lax.all_gather(core_flat, 'ep', axis=0, tiled=True)]
    all_to_all x0 -> x1, waiting for transfers between devices: none -> 13.1 us  [gather_by_exchange(): lax.all_to_all(jnp.tile(shard, repeats), axis, split_axis=dim, concat_axi...]
where the time goes in v1:
time: 557 us; the launch traced here: 551 us
  waiting for transfers between devices  170 us (31%)
  local copies, waits for them, and re-layouts  124 us (22%)
  matrix products  111 us (20%)
  blocking collectives  84.1 us (15%)
  starting transfers between devices  31.1 us (6%)
  other arithmetic  28.5 us (5%)
    all_to_all x1, blocking collectives, shards(): lax.all_to_all(outgoing.reshape(dp_size, ep_size, capacity, model_width),...  84.1 us
    dot_general x4, matrix products, delta_block(): jnp.einsum('bhkv,bhk->bhv', memory_state, queries, precision=lax.Precisio...  56.5 us
    all_to_all x1, waiting for transfers between devices, shards(): lax.all_to_all(result, 'dp', split_axis=0, concat_axis=0, tiled=True)  46.9 us
    dot_general x4, matrix products, delta_block(): jnp.einsum('bhkv,bhk->bhv', memory_state, key_units, precision=lax.Precis...  45.9 us
    all_to_all x1, waiting for transfers between devices, shards(): lax.all_to_all(pack(fresh_states, buffer_index, ep_size), 'ep', split_axi...  44.3 us
    all_to_all x1, waiting for transfers between devices, shards(): lax.all_to_all(lax.all_to_all(outgoing.reshape(dp_size, ep_size, capacity...  36.9 us
    all_to_all x1, waiting for transfers between devices, shards(): lax.all_to_all(lax.all_to_all(result, 'dp', split_axis=0, concat_axis=0,...  23.4 us
    reshape x2, local copies, waits for them, and re-layouts, shards(): expert_apply(arrived.reshape(-1, model_width), gate_up[0], down_weight[0])  16.3 us
  transfers between devices with their start and end apart: 7, of which 6 were waited for; matrix products, arithmetic and copies ran while one was open for 16% of the time, Pallas kernels for 0%

profile of v1, /device:TPU:24, one launch (start us, length us, event | category | flops | bytes accessed | tf_op | source)
XLA Modules:
  0.0 550.8 jit_solution(10348469416959453216)
XLA Ops:
  0.6 0.9 fusion.58
  1.6 0.9 fusion.59
  2.4 1.2 slice_convert_fusion.14
  4.4 1.1 slice_convert_fusion.15
  6.2 1.5 slice_convert_fusion.7
  7.7 9.7 %fusion = f32[8,16,1,128]{3,2,1,0:T(1,128)S(1)} fusion(f32[8,16,128,1]{2,3,1,0:T(1,128)S(1)} %bitcast.154, bf16[8,16,128,128]{3,2,1,0:T(8,128)(2,1)} %param.16, f32[8,16]{1,0:T(8,128)S(1)} %get-tuple-element.37), kind=kOutput, calls=%fused_computation.10 | convolution fusion | flops 29360128 | bytes 4325888 | tf_op jit(solution)/shard_map/bhkv,bhk->bhv/dot_general | solution.py:46
  17.6 8.3 %fusion.2 = f32[8,16,1,128]{3,2,1,0:T(1,128)S(1)} fusion(f32[8,16,128,1]{2,3,1,0:T(1,128)S(1)} %bitcast.198, bf16[8,16,128,128]{3,2,1,0:T(8,128)(2,1)S(1)} %copy-done.1, f32[8,16,128]{2,1,0:T(8,128)S(1)} %subtract_multiply_fusion.3, f32[8,16,128]{2,1,0:T(8,128)S(1)} %bitcast.155, f32[8,16]{1,0:T(8,128)S(1)} %get-tuple-element.37), kind=kOutput, calls=%fused_computation.12 | convolution fusion | flops 33554432 | bytes 4456960 | tf_op jit(solution)/shard_map/bhkv,bhk->bhv/dot_general | solution.py:51
  26.0 9.0 %fusion.3 = f32[8,16,1,128]{3,2,1,0:T(1,128)S(1)} fusion(f32[8,16,128,1]{2,3,1,0:T(1,128)S(1)} %bitcast.163, bf16[8,16,128,128]{3,2,1,0:T(8,128)(2,1)S(1)} %copy-done.1, f32[8,16]{1,0:T(8,128)S(1)} %get-tuple-element.36, f32[8,16,128]{2,1,0:T(8,128)S(1)} %subtract_multiply_fusion.3, f32[8,16,128]{2,1,0:T(8,128)S(1)} %bitcast.156, ...), kind=kOutput, calls=%fused_computation.13 | convolution fusion | flops 35651584 | bytes 4457472 | tf_op jit(solution)/shard_map/bhkv,bhk->bhv/dot_general | solution.py:46
  35.1 11.6 %fusion.11 = f32[8,16,1,128]{3,2,1,0:T(1,128)S(1)} fusion(f32[8,16,128,1]{2,3,1,0:T(1,128)S(1)} %bitcast.199, bf16[8,16,128,128]{3,2,1,0:T(8,128)(2,1)S(1)} %copy-done.1, f32[8,16,128]{2,1,0:T(8,128)S(1)} %subtract_multiply_fusion.2, f32[8,16,128]{2,1,0:T(8,128)S(1)} %bitcast.164, f32[8,16]{1,0:T(8,128)S(1)} %get-tuple-element.36, ...), kind=kOutput, calls=%fused_computation.20 | convolution fusion | flops 39845888 | bytes 4588544 | tf_op jit(solution)/shard_map/bhkv,bhk->bhv/dot_general | solution.py:51
  46.9 11.7 %fusion.7 = f32[8,16,1,128]{3,2,1,0:T(1,128)S(1)} fusion(f32[8,16,128,1]{2,3,1,0:T(1,128)S(1)} %bitcast.170, bf16[8,16,128,128]{3,2,1,0:T(8,128)(2,1)S(1)} %copy-done.1, f32[8,16]{1,0:T(8,128)S(1)} %get-tuple-element.35, f32[8,16,128]{2,1,0:T(8,128)S(1)} %subtract_multiply_fusion.2, f32[8,16,128]{2,1,0:T(8,128)S(1)} %bitcast.165, ...), kind=kOutput, calls=%fused_computation.16 | convolution fusion | flops 41943040 | bytes 4589056 | tf_op jit(solution)/shard_map/bhkv,bhk->bhv/dot_general | solution.py:46
  58.7 15.5 %fusion.43 = f32[8,16,1,128]{3,2,1,0:T(1,128)S(1)} fusion(f32[8,16,128,1]{2,3,1,0:T(1,128)S(1)} %bitcast.200, bf16[8,16,128,128]{3,2,1,0:T(8,128)(2,1)S(1)} %copy-done.1, f32[8,16,128]{2,1,0:T(8,128)S(1)} %subtract_multiply_fusion.1, f32[8,16,128]{2,1,0:T(8,128)S(1)} %bitcast.171, f32[8,16]{1,0:T(8,128)S(1)} %get-tuple-element.35, ...), kind=kOutput, calls=%fused_computation.56 | convolution fusion | flops 46137344 | bytes 4720128 | tf_op jit(solution)/shard_map/bhkv,bhk->bhv/dot_general | solution.py:51
  74.3 15.6 %fusion.5 = f32[8,16,1,128]{3,2,1,0:T(1,128)S(1)} fusion(f32[8,16,128,1]{2,3,1,0:T(1,128)S(1)} %bitcast.175, f32[8,16]{1,0:T(8,128)S(1)} %get-tuple-element.34, bf16[8,16,128,128]{3,2,1,0:T(8,128)(2,1)S(1)} %copy-done.1, f32[8,16,128]{2,1,0:T(8,128)S(1)} %subtract_multiply_fusion.1, f32[8,16,128]{2,1,0:T(8,128)S(1)} %bitcast.172, ...), kind=kOutput, calls=%fused_computation.14 | convolution fusion | flops 48234496 | bytes 4720640 | tf_op jit(solution)/shard_map/bhkv,bhk->bhv/dot_general | solution.py:46
  90.2 21.1 %fusion.10 = f32[8,16,1,128]{3,2,1,0:T(1,128)S(1)} fusion(f32[8,16,128,1]{2,3,1,0:T(1,128)S(1)} %bitcast.201, f32[8,16,128]{2,1,0:T(8,128)S(1)} %subtract_multiply_fusion, f32[8,16,128]{2,1,0:T(8,128)S(1)} %bitcast.176, f32[8,16]{1,0:T(8,128)S(1)} %get-tuple-element.34, bf16[8,16,128,128]{3,2,1,0:T(8,128)(2,1)S(1)} %copy-done.1, ...), kind=kOutput, calls=%fused_computation.19 | convolution fusion | flops 52428800 | bytes 4851712 | tf_op jit(solution)/shard_map/bhkv,bhk->bhv/dot_general | solution.py:51
  111.5 0.2 slice_convert_fusion.6
  112.1 1.1 tile.9
  113.2 4.4 all-to-all-start
  117.9 0.3 fusion.44
  118.2 0.8 copy-done.4
  119.0 1.1 broadcast_add_fusion
  120.2 0.2 fusion.48
  120.5 13.1 %all-to-all-done = bf16[8,32,2048]{2,1,0:T(8,128)(2,1)S(1)} async-done(((bf16[8,32,2048]{2,1,0:T(8,128)(2,1)}), bf16[8,32,2048]{2,1,0:T(8,128)(2,1)S(1)}, u32[]{:S(2)}, u32[]{:S(2)}) %all-to-all-start) | async-done | bytes 1048608 | tf_op jit(solution)/shard_map/all_to_all | solution.py:12
  133.6 2.3 convolution_convert_fusion.1
  135.9 3.5 all-to-all-start.1
  139.6 0.6 fusion.52
  140.2 5.3 all-to-all-done.1
  146.2 0.8 multiply_convert_fusion
  147.0 1.6 broadcast_in_dim.31
  148.5 3.6 reshape.563
  152.1 5.4 scatter_custom_fusion
  157.5 9.1 %reshape.507 = bf16[32,8,3,2048]{3,2,1,0:T(4,128)(2,1)} reshape(bf16[768,2048]{1,0:T(8,128)(2,1)} %scatter_custom_fusion) | data formatting | bytes 6291456 | tf_op jit(solution)/shard_map/reshape | solution.py:151
  166.6 5.5 copy.104
  172.1 84.1 %all_to_all.59 = bf16[32,8,3,2048]{3,1,2,0:T(8,128)(2,1)S(1)} all-to-all(bf16[32,8,3,2048]{3,1,2,0:T(8,128)(2,1)S(1)} %copy.104), channel_id=1, replica_groups=mesh['dp'=32,'ep'=8] {'dp'}, dimensions={0} | all-to-all | bytes 6291456 | tf_op jit(solution)/shard_map/all_to_all | solution.py:150
  256.2 3.4 copy.105
  259.6 4.6 all-to-all-start.3
  264.4 0.6 scatter_custom_fusion.1
  265.0 0.7 copy.110
  265.7 36.9 %all-to-all-done.3 = bf16[32,8,3,2048]{3,0,2,1:T(8,128)(2,1)} async-done(((bf16[32,8,3,2048]{3,0,2,1:T(8,128)(2,1)}), bf16[32,8,3,2048]{3,0,2,1:T(8,128)(2,1)}, u32[]{:S(2)}, u32[]{:S(2)}) %all-to-all-start.3) | async-done | bytes 3145760 | tf_op jit(solution)/shard_map/all_to_all | solution.py:149
  302.6 3.5 all-to-all-start.6
  306.1 6.6 %copy.106 = bf16[32,8,3,2048]{3,2,1,0:T(4,128)(2,1)} copy(bf16[32,8,3,2048]{3,0,2,1:T(8,128)(2,1)} %all-to-all-done.3) | data formatting | bytes 6291456 | tf_op jit(solution)/shard_map/all_to_all | solution.py:149
  312.7 8.8 %reshape.508 = bf16[768,2048]{1,0:T(8,128)(2,1)} reshape(bf16[32,8,3,2048]{3,2,1,0:T(4,128)(2,1)} %copy.106) | data formatting | bytes 6291456 | tf_op jit(solution)/shard_map/reshape | solution.py:162
  321.6 3.8 fusion.37
  325.3 2.7 convolution_convert_fusion
  328.0 9.1 %reshape.509 = bf16[32,8,3,2048]{3,2,1,0:T(4,128)(2,1)} reshape(bf16[768,2048]{1,0:T(8,128)(2,1)} %convolution_convert_fusion) | data formatting | bytes 6291456 | tf_op jit(solution)/shard_map/reshape | solution.py:162
  337.1 7.2 %copy.107 = bf16[32,8,3,2048]{3,1,2,0:T(8,128)(2,1)} copy(bf16[32,8,3,2048]{3,2,1,0:T(4,128)(2,1)} %reshape.509) | data formatting | bytes 6291456 | tf_op jit(solution)/shard_map/reshape | solution.py:162
  344.4 5.8 %all-to-all-start.4 = ((bf16[32,8,3,2048]{3,1,2,0:T(8,128)(2,1)}), bf16[32,8,3,2048]{3,1,2,0:T(8,128)(2,1)}, u32[]{:S(2)}, u32[]{:S(2)}) async-start(bf16[32,8,3,2048]{3,1,2,0:T(8,128)(2,1)} %copy.107), calls=%async_computation.4 | async-start | bytes 6291456 | tf_op jit(solution)/shard_map/all_to_all | solution.py:166
  350.3 13.3 %fusion.9 = bf16[8,16,128,128]{3,2,1,0:T(8,128)(2,1)} fusion(f32[8,16,128]{2,1,0:T(8,128)S(1)} %copy-done.14, f32[8,16,128]{2,1,0:T(8,128)S(1)} %bitcast.177, f32[8,16]{1,0:T(8,128)S(1)} %get-tuple-element.34, f32[8,16,128]{2,1,0:T(8,128)S(1)} %copy-done.12, f32[8,16,128]{2,1,0:T(8,128)S(1)} %bitcast.174, f32[8,16]{1,0:T(8,128)S(1)} %get-tuple-element.35, ...), kind=kLoop, calls=%fused_computation.18 | loop fusion | flops 29360128 | bytes 8914944 | tf_op jit(solution)/shard_map/convert_element_type | solution.py:60
  363.5 3.1 broadcast.334.clone
  366.6 10.9 %scatter_fusion = bf16[8,16,128,128]{3,2,1,0:T(8,128)(2,1)} fusion(bf16[8,16,128,128]{3,2,1,0:T(8,128)(2,1)} %broadcast.334.clone, s32[8]{0:T(128)S(1)} %compare_select_fusion.2, bf16[8,16,128,128]{3,2,1,0:T(8,128)(2,1)} %fusion.9), kind=kCustom, calls=%fused_computation.3 | custom fusion | bytes 12582944 | tf_op jit(solution)/shard_map/scatter | solution.py:76
  377.4 46.9 %all-to-all-done.4 = bf16[32,8,3,2048]{3,1,2,0:T(8,128)(2,1)} async-done(((bf16[32,8,3,2048]{3,1,2,0:T(8,128)(2,1)}), bf16[32,8,3,2048]{3,1,2,0:T(8,128)(2,1)}, u32[]{:S(2)}, u32[]{:S(2)}) %all-to-all-start.4) | async-done | bytes 3145760 | tf_op jit(solution)/shard_map/all_to_all | solution.py:166
  424.3 4.8 all-to-all-start.7
  429.1 5.3 copy.108
  434.4 44.3 %all-to-all-done.7 = bf16[8,1,16,128,128]{4,3,2,1,0:T(8,128)(2,1)} async-done(((bf16[8,1,16,128,128]{4,3,2,1,0:T(8,128)(2,1)}), bf16[8,1,16,128,128]{4,3,2,1,0:T(8,128)(2,1)}, u32[]{:S(2)}, u32[]{:S(2)}) %all-to-all-start.7) | async-done | bytes 4194336 | tf_op jit(solution)/shard_map/all_to_all | solution.py:118
  478.8 4.5 all-to-all-start.5
  483.4 0.6 pad_clamp_fusion
  484.1 0.2 reduce.3
  484.3 3.1 broadcast.334
  487.4 10.9 %scatter_fusion.1 = bf16[8,16,128,128]{3,2,1,0:T(8,128)(2,1)} fusion(bf16[8,16,128,128]{3,2,1,0:T(8,128)(2,1)} %broadcast.334, s32[8]{0:T(128)S(1)} %fusion.54, bf16[8,16,128,128]{3,2,1,0:T(8,128)(2,1)} %bitcast.78), kind=kCustom, calls=%fused_computation.4 | custom fusion | bytes 12582944 | tf_op jit(solution)/shard_map/scatter | solution.py:125
  498.2 23.4 %all-to-all-done.5 = bf16[32,8,3,2048]{3,0,2,1:T(8,128)(2,1)} async-done(((bf16[32,8,3,2048]{3,0,2,1:T(8,128)(2,1)}), bf16[32,8,3,2048]{3,0,2,1:T(8,128)(2,1)}, u32[]{:S(2)}, u32[]{:S(2)}) %all-to-all-start.5) | async-done | bytes 3145760 | tf_op jit(solution)/shard_map/all_to_all | solution.py:165
  521.7 6.5 %copy.109 = bf16[32,8,3,2048]{3,2,1,0:T(4,128)(2,1)} copy(bf16[32,8,3,2048]{3,0,2,1:T(8,128)(2,1)} %all-to-all-done.5) | data formatting | bytes 6291456 | tf_op jit(solution)/shard_map/all_to_all | solution.py:165
  528.2 8.8 %reshape.510 = bf16[768,2048]{1,0:T(8,128)(2,1)} reshape(bf16[32,8,3,2048]{3,2,1,0:T(4,128)(2,1)} %copy.109) | data formatting | bytes 6291456 | tf_op jit(solution)/shard_map/reshape | solution.py:172
  537.0 6.8 %gather_fusion = bf16[320,2048]{1,0:T(8,128)(2,1)S(1)} fusion(bf16[768,2048]{1,0:T(8,128)(2,1)} %reshape.510, s32[1024]{0:T(1024)} %pad_clamp_fusion), kind=kCustom, calls=%fused_computation | custom fusion | bytes 2622720 | tf_op jit(solution)/shard_map/gather | solution.py:172
  543.8 2.1 reshape.550
  545.9 3.6 multiply_reduce_fusion
  549.6 0.8 fusion.50
  (139 shorter events, 4.5 us)
Async XLA Ops:
  0.6 320.9 %copy-start = (bf16[1,2048,512]{2,1,0:T(8,128)(2,1)S(1)}, bf16[1,2048,512]{2,1,0:T(8,128)(2,1)}, u32[]{:S(2)}) copy-start(bf16[1,2048,512]{2,1,0:T(8,128)(2,1)} %param.29) | copy-start | bytes 6291460
  2.4 15.1 %copy-start.1 = (bf16[8,16,128,128]{3,2,1,0:T(8,128)(2,1)S(1)}, bf16[8,16,128,128]{3,2,1,0:T(8,128)(2,1)}, u32[]{:S(2)}) copy-start(bf16[8,16,128,128]{3,2,1,0:T(8,128)(2,1)} %param.16) | copy-start | bytes 12582916
  7.7 82.4 %copy-start.15 = (f32[8,8,2,128]{3,2,1,0:T(2,128)}, f32[8,8,2,128]{3,2,1,0:T(2,128)S(1)}, u32[]{:S(2)}) copy-start(f32[8,8,2,128]{3,2,1,0:T(2,128)S(1)} %broadcast_in_dim.22) | copy-start | bytes 196612
  17.5 72.6 %copy-start.7 = (f32[8,16,128]{2,1,0:T(8,128)}, f32[8,16,128]{2,1,0:T(8,128)S(1)}, u32[]{:S(2)}) copy-start(f32[8,16,128]{2,1,0:T(8,128)S(1)} %subtract_multiply_fusion.3) | copy-start | bytes 196612
  26.0 64.1 %copy-start.17 = (f32[8,8,2,128]{3,2,1,0:T(2,128)}, f32[8,8,2,128]{3,2,1,0:T(2,128)S(1)}, u32[]{:S(2)}) copy-start(f32[8,8,2,128]{3,2,1,0:T(2,128)S(1)} %broadcast_in_dim.24) | copy-start | bytes 196612
  35.1 55.1 %copy-start.9 = (f32[8,16,128]{2,1,0:T(8,128)}, f32[8,16,128]{2,1,0:T(8,128)S(1)}, u32[]{:S(2)}) copy-start(f32[8,16,128]{2,1,0:T(8,128)S(1)} %subtract_multiply_fusion.2) | copy-start | bytes 196612
  46.9 43.3 %copy-start.19 = (f32[8,8,2,128]{3,2,1,0:T(2,128)}, f32[8,8,2,128]{3,2,1,0:T(2,128)S(1)}, u32[]{:S(2)}) copy-start(f32[8,8,2,128]{3,2,1,0:T(2,128)S(1)} %broadcast_in_dim.26) | copy-start | bytes 196612
  58.6 31.5 %copy-start.11 = (f32[8,16,128]{2,1,0:T(8,128)}, f32[8,16,128]{2,1,0:T(8,128)S(1)}, u32[]{:S(2)}) copy-start(f32[8,16,128]{2,1,0:T(8,128)S(1)} %subtract_multiply_fusion.1) | copy-start | bytes 196612
  74.3 15.8 %copy-start.21 = (f32[8,8,2,128]{3,2,1,0:T(2,128)}, f32[8,8,2,128]{3,2,1,0:T(2,128)S(1)}, u32[]{:S(2)}) copy-start(f32[8,8,2,128]{3,2,1,0:T(2,128)S(1)} %broadcast_in_dim.28) | copy-start | bytes 196612
  90.1 21.3 %copy-start.13 = (f32[8,16,128]{2,1,0:T(8,128)}, f32[8,16,128]{2,1,0:T(8,128)S(1)}, u32[]{:S(2)}) copy-start(f32[8,16,128]{2,1,0:T(8,128)S(1)} %subtract_multiply_fusion) | copy-start | bytes 196612
  90.2 21.3 %copy-start.6 = (bf16[8,4,2048]{2,1,0:T(4,128)(2,1)S(1)}, bf16[8,4,2048]{2,1,0:T(4,128)(2,1)}, u32[]{:S(2)}) copy-start(bf16[8,4,2048]{2,1,0:T(4,128)(2,1)} %param.20) | copy-start | bytes 393220
  90.2 21.5 %copy-start.26 = (f32[128]{0:T(128)S(1)}, f32[128]{0:T(128)}, u32[]{:S(2)}) copy-start(f32[128]{0:T(128)} %param.27) | copy-start | bytes 1540
  111.3 6.3 %copy-start.23 = (s32[8,4,10]{2,1,0:T(4,128)S(1)}, s32[8,4,10]{2,1,0:T(4,128)}, u32[]{:S(2)}) copy-start(s32[8,4,10]{2,1,0:T(4,128)} %param.24) | copy-start | bytes 3844
  113.2 26.4 %copy-start.5 = (bf16[8,4,2048]{2,1,0:T(4,128)(2,1)S(1)}, bf16[8,4,2048]{2,1,0:T(4,128)(2,1)}, u32[]{:S(2)}) copy-start(bf16[8,4,2048]{2,1,0:T(4,128)(2,1)} %param.23) | copy-start | bytes 393220
  113.2 20.4 %all-to-all-start = ((bf16[8,32,2048]{2,1,0:T(8,128)(2,1)}), bf16[8,32,2048]{2,1,0:T(8,128)(2,1)S(1)}, u32[]{:S(2)}, u32[]{:S(2)}) async-start(bf16[8,32,2048]{2,1,0:T(8,128)(2,1)} %tile.9), calls=%async_computation | async-start | bytes 2097152 | tf_op jit(solution)/shard_map/all_to_all | solution.py:12
  118.2 0.8 copy-start.4
  135.9 9.6 %all-to-all-start.1 = ((bf16[8,32,256]{2,1,0:T(8,128)(2,1)}), bf16[8,32,256]{2,1,0:T(8,128)(2,1)S(1)}, u32[]{:S(2)}, u32[]{:S(2)}) async-start(bf16[8,32,256]{2,1,0:T(8,128)(2,1)} %bitcast.65), calls=%async_computation.1 | async-start | bytes 262144 | tf_op jit(solution)/shard_map/all_to_all | solution.py:131
  145.9 11.7 %copy-start.2 = (f32[8,4,2048]{2,1,0:T(4,128)}, f32[8,4,2048]{2,1,0:T(4,128)S(1)}, u32[]{:S(2)}) copy-start(f32[8,4,2048]{2,1,0:T(4,128)S(1)} %reshape.546) | copy-start | bytes 786436
  259.6 4.6 copy-start.28
  259.6 43.0 %all-to-all-start.3 = ((bf16[32,8,3,2048]{3,0,2,1:T(8,128)(2,1)}), bf16[32,8,3,2048]{3,0,2,1:T(8,128)(2,1)}, u32[]{:S(2)}, u32[]{:S(2)}) async-start(bf16[32,8,3,2048]{3,0,2,1:T(8,128)(2,1)} %copy.105), calls=%async_computation.3 | async-start | bytes 6291456 | tf_op jit(solution)/shard_map/all_to_all | solution.py:149
  302.6 41.8 %all-to-all-start.6 = ((s32[8,1,1]{2,1,0:T(1,128)}), s32[8,1,1]{2,1,0:T(1,128)S(1)}, u32[]{:S(2)}, u32[]{:S(2)}) async-start(s32[8,1,1]{2,1,0:T(1,128)} %copy.110), calls=%async_computation.6 | async-start | bytes 8192 | tf_op jit(solution)/shard_map/all_to_all | solution.py:121
  321.6 3.8 copy-start.27
  344.3 5.8 %copy-start.8 = (f32[8,16,128]{2,1,0:T(8,128)S(1)}, f32[8,16,128]{2,1,0:T(8,128)}, u32[]{:S(2)}) copy-start(f32[8,16,128]{2,1,0:T(8,128)} %copy-done.7) | copy-start | bytes 196612
  344.3 5.8 %copy-start.10 = (f32[8,16,128]{2,1,0:T(8,128)S(1)}, f32[8,16,128]{2,1,0:T(8,128)}, u32[]{:S(2)}) copy-start(f32[8,16,128]{2,1,0:T(8,128)} %copy-done.9) | copy-start | bytes 196612
  344.3 5.8 %copy-start.12 = (f32[8,16,128]{2,1,0:T(8,128)S(1)}, f32[8,16,128]{2,1,0:T(8,128)}, u32[]{:S(2)}) copy-start(f32[8,16,128]{2,1,0:T(8,128)} %copy-done.11) | copy-start | bytes 196612
  344.4 5.9 %copy-start.14 = (f32[8,16,128]{2,1,0:T(8,128)S(1)}, f32[8,16,128]{2,1,0:T(8,128)}, u32[]{:S(2)}) copy-start(f32[8,16,128]{2,1,0:T(8,128)} %copy-done.13) | copy-start | bytes 196612
  344.4 5.9 %copy-start.16 = (f32[8,8,2,128]{3,2,1,0:T(2,128)S(1)}, f32[8,8,2,128]{3,2,1,0:T(2,128)}, u32[]{:S(2)}) copy-start(f32[8,8,2,128]{3,2,1,0:T(2,128)} %copy-done.15) | copy-start | bytes 196612
  344.4 5.9 %copy-start.18 = (f32[8,8,2,128]{3,2,1,0:T(2,128)S(1)}, f32[8,8,2,128]{3,2,1,0:T(2,128)}, u32[]{:S(2)}) copy-start(f32[8,8,2,128]{3,2,1,0:T(2,128)} %copy-done.17) | copy-start | bytes 196612
  344.4 5.9 %copy-start.20 = (f32[8,8,2,128]{3,2,1,0:T(2,128)S(1)}, f32[8,8,2,128]{3,2,1,0:T(2,128)}, u32[]{:S(2)}) copy-start(f32[8,8,2,128]{3,2,1,0:T(2,128)} %copy-done.19) | copy-start | bytes 196612
  344.4 5.9 %copy-start.22 = (f32[8,8,2,128]{3,2,1,0:T(2,128)S(1)}, f32[8,8,2,128]{3,2,1,0:T(2,128)}, u32[]{:S(2)}) copy-start(f32[8,8,2,128]{3,2,1,0:T(2,128)} %copy-done.21) | copy-start | bytes 196612
  344.4 79.9 %all-to-all-start.4 = ((bf16[32,8,3,2048]{3,1,2,0:T(8,128)(2,1)}), bf16[32,8,3,2048]{3,1,2,0:T(8,128)(2,1)}, u32[]{:S(2)}, u32[]{:S(2)}) async-start(bf16[32,8,3,2048]{3,1,2,0:T(8,128)(2,1)} %copy.107), calls=%async_computation.4 | async-start | bytes 6291456 | tf_op jit(solution)/shard_map/all_to_all | solution.py:166
  424.3 54.5 %all-to-all-start.7 = ((bf16[8,1,16,128,128]{4,3,2,1,0:T(8,128)(2,1)}), bf16[8,1,16,128,128]{4,3,2,1,0:T(8,128)(2,1)}, u32[]{:S(2)}, u32[]{:S(2)}) async-start(bf16[8,1,16,128,128]{4,3,2,1,0:T(8,128)(2,1)} %bitcast.133), calls=%async_computation.7 | async-start | bytes 8388608 | tf_op jit(solution)/shard_map/all_to_all | solution.py:118
  434.4 48.8 %copy-start.24 = (f32[8,4,10]{2,1,0:T(4,128)S(1)}, f32[8,4,10]{2,1,0:T(4,128)}, u32[]{:S(2)}) copy-start(f32[8,4,10]{2,1,0:T(4,128)} %param.25) | copy-start | bytes 3844
  434.4 49.0 %copy-start.25 = (s32[320]{0:T(512)S(1)}, s32[320]{0:T(512)}, u32[]{:S(2)}) copy-start(s32[320]{0:T(512)} %fusion.52) | copy-start | bytes 3844
  478.8 42.9 %all-to-all-start.5 = ((bf16[32,8,3,2048]{3,0,2,1:T(8,128)(2,1)}), bf16[32,8,3,2048]{3,0,2,1:T(8,128)(2,1)}, u32[]{:S(2)}, u32[]{:S(2)}) async-start(bf16[32,8,3,2048]{3,0,2,1:T(8,128)(2,1)} %copy.108), calls=%async_computation.5 | async-start | bytes 6291456 | tf_op jit(solution)/shard_map/all_to_all | solution.py:165
  545.9 3.7 copy-start.3
